TPU v7x, 32 devices: a whole 2x2x4 slice. The times are simulated.
32 devices in a mesh: slab: 8 (over y, x, core), grp: 4 (over z).
Axes of the slice: x: 2, y: 2, z: 4, core: 2. Of those that a mesh axis runs over, the one named last changes fastest.
Arguments:
- volume: float32 [64, 32, 16, 128], P(None, 'slab', 'grp'), may hold values from -6 to 6
- conv_fine: float32 [3, 3, 3, 64, 64], replicated, may hold values from -0.15625 to 0.15625
- down_first: float32 [2, 2, 2, 64, 128], replicated, may hold values from -0.25 to 0.25
- conv_middle: float32 [3, 3, 3, 128, 128], replicated, may hold values from -0.109375 to 0.109375
- down_second: float32 [2, 2, 2, 128, 256], P(None, None, None, None, 'grp'), may hold values from -0.1875 to 0.1875
- conv_coarse: float32 [3, 3, 3, 256, 512], P(None, None, None, None, 'grp'), may hold values from -0.078125 to 0.078125
Outputs:
- features: float32 [512, 8, 128], P('grp', 'slab')
All inputs are finite; a program needn't handle non-finite values.
Results may differ from a plain program's by a relative error of at most 0.000082.
Values sent between devices are 32-bit elements; how exact they have to be, the bound alone decides.
A program may use at most 64 MiB of HBM per device.

v0:
```python
import jax
import jax.numpy as jnp
from jax import lax
from jax.sharding import PartitionSpec as P


def padded_2(cells, sides, width):
    for axis, dim in sides:
        count = lax.axis_size(axis)
        ends = count - 1
        head = lax.slice_in_dim(cells, 0, width, axis=dim)
        tail = lax.slice_in_dim(cells, cells.shape[dim] - width, cells.shape[dim], axis=dim)
        cells = jnp.concatenate(
            [
                lax.ppermute(tail, axis, [(i, (i + 1) % count) for i in range(ends)]),
                cells,
                lax.ppermute(head, axis, [((i + 1) % count, i) for i in range(ends)]),
            ],
            axis=dim,
        )
    return cells


def from_behind(shard, axis, by):
    peers = lax.axis_size(axis)
    pairs = [(i, i + by) for i in range(peers) if 0 <= i + by < peers]
    return lax.ppermute(shard, axis, pairs)


def convolve(field, kernel, stride, padding):
    return lax.conv_general_dilated(
        field[None],
        kernel,
        (stride, stride, stride),
        padding,
        dimension_numbers=("NCDHW", "DHWIO", "NCDHW"),
        precision=lax.Precision.HIGH,
    )[0]


def per_device(volume, conv_fine, down_first, conv_middle, down_second, conv_coarse):
    valid = ((0, 0), (0, 0), (0, 0))
    sideways = ((0, 0), (0, 0), (1, 1))
    padded = padded_2(volume, (("slab", 1), ("grp", 2)), 1)
    level_one = jax.nn.gelu(convolve(padded, conv_fine, 1, sideways), approximate=False)
    level_two = convolve(level_one, down_first, 2, valid)
    padded_two = padded_2(level_two, (("slab", 1), ("grp", 2)), 1)
    level_two = jax.nn.gelu(convolve(padded_two, conv_middle, 1, sideways), approximate=False)
    gathered = lax.all_gather(level_two, "grp", axis=2, tiled=True)
    shares = convolve(gathered, down_second, 2, valid)
    coarse = lax.all_gather(shares, "grp", axis=0, tiled=True)
    planar = ((0, 0), (1, 1), (1, 1))
    summed = convolve(coarse, conv_coarse, 1, ((1, 1), (1, 1), (1, 1)))
    upward = convolve(coarse[:, -1:], conv_coarse[0:1], 1, planar)
    downward = convolve(coarse[:, :1], conv_coarse[2:3], 1, planar)
    from_lower = from_behind(upward, "slab", 1)
    from_upper = from_behind(downward, "slab", -1)
    summed = summed.at[:, :1].add(from_lower)
    summed = summed.at[:, -1:].add(from_upper)
    result = jax.nn.gelu(summed, approximate=False)
    return result.reshape(result.shape[0], result.shape[1], result.shape[2] * result.shape[3])


def solution(mesh):
    placed = (
        P(None, "slab", "grp", None),
        P(),
        P(),
        P(),
        P(None, None, None, None, "grp"),
        P(None, None, None, None, "grp"),
    )
    return jax.shard_map(
        per_device, mesh=mesh, in_specs=placed, out_specs=P("grp", "slab", None), check_vma=False
    )
```

profile of v0, /device:TPU:3, one launch (start us, length us, event | category | flops | bytes accessed | tf_op | source)
XLA Modules:
  0.0 111.9 jit_solution(5088710529204012672)
XLA Ops:
  1.2 3.7 %collective-permute-start = (f32[64,1,4,128]{3,0,2,1:T(8,128)S(1)}, f32[64,1,4,128]{3,0,2,1:T(8,128)S(1)}, u32[]{:S(2)}, u32[]{:S(2)}) collective-permute-start(f32[64,1,4,128]{3,0,2,1:T(8,128)S(1)} %copy.117), channel_id=1, source_target_pairs={{0,4},{4,8},{8,12},{12,16},{16,20},{20,24},{24,28},{1,5},{5,9},{9,... | collective-permute-start | bytes 393224 | tf_op jit(solution)/shard_map/ppermute | solution.py:15
  4.9 1.9 %collective-permute-start.1 = (f32[64,1,4,128]{3,0,2,1:T(8,128)S(1)}, f32[64,1,4,128]{3,0,2,1:T(8,128)S(1)}, u32[]{:S(2)}, u32[]{:S(2)}) collective-permute-start(f32[64,1,4,128]{3,0,2,1:T(8,128)S(1)} %copy.118), channel_id=1, source_target_pairs={{4,0},{8,4},{12,8},{16,12},{20,16},{24,20},{28,24},{5,1},{9,5},{13... | collective-permute-start | bytes 393224 | tf_op jit(solution)/shard_map/ppermute | solution.py:17
  7.0 5.1 %collective-permute-done.1 = f32[64,1,4,128]{3,0,2,1:T(8,128)S(1)} collective-permute-done((f32[64,1,4,128]{3,0,2,1:T(8,128)S(1)}, f32[64,1,4,128]{3,0,2,1:T(8,128)S(1)}, u32[]{:S(2)}, u32[]{:S(2)}) %collective-permute-start.1) | collective-permute-done | bytes 131104 | tf_op jit(solution)/shard_map/ppermute | solution.py:17
  12.1 3.2 %collective-permute-start.2 = (f32[64,6,1,128]{3,0,2,1:T(8,128)S(1)}, f32[64,6,1,128]{3,0,2,1:T(8,128)S(1)}, u32[]{:S(2)}, u32[]{:S(2)}) collective-permute-start(f32[64,6,1,128]{3,0,2,1:T(8,128)S(1)} %get-tuple-element.45), channel_id=1, source_target_pairs={{0,1},{1,2},{2,3},{4,5},{5,6},{6,7},{8,9},{9,10},{10,11},{12,13},{... | collective-permute-start | bytes 589832 | tf_op jit(solution)/shard_map/ppermute | solution.py:15
  16.6 1.7 %collective-permute-done.2 = f32[64,6,1,128]{3,0,2,1:T(8,128)S(1)} collective-permute-done((f32[64,6,1,128]{3,0,2,1:T(8,128)S(1)}, f32[64,6,1,128]{3,0,2,1:T(8,128)S(1)}, u32[]{:S(2)}, u32[]{:S(2)}) %collective-permute-start.2) | collective-permute-done | bytes 196640 | tf_op jit(solution)/shard_map/ppermute | solution.py:15
  18.4 4.1 %collective-permute-done.3 = f32[64,6,1,128]{3,0,2,1:T(8,128)S(1)} collective-permute-done((f32[64,6,1,128]{3,0,2,1:T(8,128)S(1)}, f32[64,6,1,128]{3,0,2,1:T(8,128)S(1)}, u32[]{:S(2)}, u32[]{:S(2)}) %collective-permute-start.3) | collective-permute-done | bytes 196640 | tf_op jit(solution)/shard_map/ppermute | solution.py:17
  22.6 4.2 %copy.106 = f32[64,6,6,1,128]{0,3,4,2,1:T(1,128)} copy(f32[64,6,6,1,128]{4,0,2,1,3:T(8,128)S(1)} %maximum_bitcast_fusion) | data formatting | bytes 2359296
  26.8 3.4 %pad.6.clone = f32[64,6,6,1,136]{0,3,4,2,1:T(1,128)S(1)} pad(f32[64,6,6,1,128]{0,3,4,2,1:T(1,128)} %copy.106, f32[]{:T(128)} %constant.74.clone.1), padding=0_0x0_0x0_0x0_0x1_7 | pad | bytes 2433028 | tf_op jit(solution)/shard_map/broadcast_in_dim | solution.py:32
  31.4 8.9 %fusion.22 = f32[4,4,8,17,64]{4,2,3,1,0:T(8,128)S(1)} fusion(f32[3,3,3,64,64]{4,3,2,1,0:T(8,128)S(1)} %copy-done.7, f32[64,6,6,1,7,2]{0,4,5,2,1,3:T(8,128)S(1)} %slice.107, f32[64,6,6,1,8,17]{0,4,5,2,1,3:T(8,128)S(1)} %copy.71, pred[8,17]{0,1:T(8,128)(4,1)S(1)} %copy-done.8), kind=kOutput, calls=%fused_computation.21 | convolution fusion | flops 1454131200 | bytes 2381960 | tf_op jit(solution)/shard_map/conv_general_dilated | solution.py:31
  42.2 4.2 %collective-permute-start.4 = (f32[128,1,2,64]{0,3,2,1:T(8,128)S(1)}, f32[128,1,2,64]{0,3,2,1:T(8,128)S(1)}, u32[]{:S(2)}, u32[]{:S(2)}) collective-permute-start(f32[128,1,2,64]{0,3,2,1:T(8,128)S(1)} %get-tuple-element.53), channel_id=1, source_target_pairs={{0,4},{4,8},{8,12},{12,16},{16,20},{20,24},{24,28},{1,5},{5,9},{9,... | collective-permute-start | bytes 196616 | tf_op jit(solution)/shard_map/ppermute | solution.py:15
  46.4 1.9 %collective-permute-start.5 = (f32[128,1,2,64]{0,3,2,1:T(8,128)S(1)}, f32[128,1,2,64]{0,3,2,1:T(8,128)S(1)}, u32[]{:S(2)}, u32[]{:S(2)}) collective-permute-start(f32[128,1,2,64]{0,3,2,1:T(8,128)S(1)} %get-tuple-element.54), channel_id=1, source_target_pairs={{4,0},{8,4},{12,8},{16,12},{20,16},{24,20},{28,24},{5,1},{9,5},{13... | collective-permute-start | bytes 196616 | tf_op jit(solution)/shard_map/ppermute | solution.py:17
  48.3 4.5 %collective-permute-done.5 = f32[128,1,2,64]{0,3,2,1:T(8,128)S(1)} collective-permute-done((f32[128,1,2,64]{0,3,2,1:T(8,128)S(1)}, f32[128,1,2,64]{0,3,2,1:T(8,128)S(1)}, u32[]{:S(2)}, u32[]{:S(2)}) %collective-permute-start.5) | collective-permute-done | bytes 65568 | tf_op jit(solution)/shard_map/ppermute | solution.py:17
  52.9 3.2 %collective-permute-start.6 = (f32[128,4,1,64]{0,3,2,1:T(8,128)S(1)}, f32[128,4,1,64]{0,3,2,1:T(8,128)S(1)}, u32[]{:S(2)}, u32[]{:S(2)}) collective-permute-start(f32[128,4,1,64]{0,3,2,1:T(8,128)S(1)} %get-tuple-element.49), channel_id=1, source_target_pairs={{0,1},{1,2},{2,3},{4,5},{5,6},{6,7},{8,9},{9,10},{10,11},{12,13},{... | collective-permute-start | bytes 393224 | tf_op jit(solution)/shard_map/ppermute | solution.py:15
  56.2 1.3 %collective-permute-start.7 = (f32[128,4,1,64]{0,3,2,1:T(8,128)S(1)}, f32[128,4,1,64]{0,3,2,1:T(8,128)S(1)}, u32[]{:S(2)}, u32[]{:S(2)}) collective-permute-start(f32[128,4,1,64]{0,3,2,1:T(8,128)S(1)} %get-tuple-element.50), channel_id=1, source_target_pairs={{1,0},{2,1},{3,2},{5,4},{6,5},{7,6},{9,8},{10,9},{11,10},{13,12},{... | collective-permute-start | bytes 393224 | tf_op jit(solution)/shard_map/ppermute | solution.py:17
  58.1 3.8 %collective-permute-done.7 = f32[128,4,1,64]{0,3,2,1:T(8,128)S(1)} collective-permute-done((f32[128,4,1,64]{0,3,2,1:T(8,128)S(1)}, f32[128,4,1,64]{0,3,2,1:T(8,128)S(1)}, u32[]{:S(2)}, u32[]{:S(2)}) %collective-permute-start.7) | collective-permute-done | bytes 131104 | tf_op jit(solution)/shard_map/ppermute | solution.py:17
  62.9 1.7 %negate_multiply_fusion.1 = (f32[2,2,8,9,128]{4,2,3,1,0:T(8,128)S(1)}, f32[2,2,8,9,128]{4,2,3,1,0:T(8,128)S(1)}) fusion(f32[3,3,3,128,128]{4,3,2,1,0:T(8,128)S(1)} %copy-done, f32[128,4,4,1,7,2]{0,4,5,2,1,3:T(8,128)S(1)} %slice.114, f32[128,4,4,1,8,9]{0,4,5,2,1,3:T(8,128)S(1)} %copy.79, pred[8,9]{0,1:T(8,128)(4,1)S(1)} %copy-done.6), kind=kOutput, calls=%fused_computation.66 | convolution fusion | flops 765100032 | bytes 2768968 | tf_op jit(solution)/shard_map/conv_general_dilated | solution.py:31
  65.2 13.8 %all_gather.6 = f32[128,2,8,64]{0,3,1,2:T(8,128)S(1)} all-gather(f32[128,2,2,64]{0,3,1,2:T(8,128)S(1)} %copy.84), channel_id=1, replica_groups=mesh['slab'=8,'grp'=4] {'grp'}, dimensions={2}, use_global_device_ids=true | all-gather | bytes 655360 | tf_op jit(solution)/shard_map/all_gather | solution.py:49
  79.7 12.8 %all-gather = f32[1,256,1,4,32]{4,3,2,0,1:T(4,128)S(1)} all-gather(f32[1,64,1,4,32]{4,3,2,0,1:T(4,128)S(1)} %copy.89), channel_id=2, replica_groups=mesh['slab'=8,'grp'=4] {'grp'}, dimensions={1}, use_global_device_ids=true | all-gather | bytes 163840 | tf_op jit(solution)/shard_map/all_gather | solution.py:51
  92.8 2.2 %fusion.14 = f32[1,4,8,5,128]{4,2,3,1,0:T(8,128)S(1)} fusion(f32[3,3,3,256,128]{4,3,2,1,0:T(8,128)} %param.19, f32[256,1,4,1,7,2]{0,4,5,2,3,1:T(8,128)S(1)} %slice.118, f32[256,1,4,1,8,5]{0,4,5,2,3,1:T(8,128)S(1)} %copy.92, pred[8,5]{0,1:T(8,128)(4,1)S(1)} %copy-done.5), kind=kOutput, calls=%fused_computation.16 | convolution fusion | flops 236122112 | bytes 1482792 | tf_op jit(solution)/shard_map/conv_general_dilated | solution.py:31
  94.9 2.0 %fusion.17 = f32[1,4,8,5,128]{4,2,3,1,0:T(8,128)S(1)} fusion(f32[3,3,3,256,128]{4,3,2,1,0:T(8,128)} %param.19, f32[256,1,4,1,7,2]{0,4,5,2,3,1:T(8,128)S(1)} %slice.118, f32[256,1,4,1,8,5]{0,4,5,2,3,1:T(8,128)S(1)} %copy.92, pred[8,5]{0,1:T(8,128)(4,1)S(1)} %copy-done.5), kind=kOutput, calls=%fused_computation.17 | convolution fusion | flops 236122112 | bytes 1482792 | tf_op jit(solution)/shard_map/conv_general_dilated | solution.py:31
  97.0 7.3 %collective-permute-start.8 = (f32[128,1,4,32]{0,2,3,1:T(4,128)S(1)}, f32[128,1,4,32]{0,2,3,1:T(4,128)S(1)}, u32[]{:S(2)}, u32[]{:S(2)}) collective-permute-start(f32[128,1,4,32]{0,2,3,1:T(4,128)S(1)} %slice_bitcast_fusion.1), channel_id=1, source_target_pairs={{0,4},{4,8},{8,12},{12,16},{16,20},{20,24},{24,28},{1,5},{5,9},{9,... | collective-permute-start | bytes 196616 | tf_op jit(solution)/shard_map/ppermute | solution.py:27
  104.4 1.9 %collective-permute-start.9 = (f32[128,1,4,32]{0,2,3,1:T(4,128)S(1)}, f32[128,1,4,32]{0,2,3,1:T(4,128)S(1)}, u32[]{:S(2)}, u32[]{:S(2)}) collective-permute-start(f32[128,1,4,32]{0,2,3,1:T(4,128)S(1)} %slice_bitcast_fusion), channel_id=1, source_target_pairs={{4,0},{8,4},{12,8},{16,12},{20,16},{24,20},{28,24},{5,1},{9,5},{13... | collective-permute-start | bytes 196616 | tf_op jit(solution)/shard_map/ppermute | solution.py:27
  106.3 2.0 %convolution_select_fusion.1 = f32[1,4,8,5,128]{4,2,3,1,0:T(8,128)S(1)} fusion(f32[3,3,3,256,128]{4,3,2,1,0:T(8,128)S(1)} %copy-done.1, f32[256,1,4,1,7,2]{0,4,5,2,3,1:T(8,128)S(1)} %slice.118, f32[256,1,4,1,8,5]{0,4,5,2,3,1:T(8,128)S(1)} %copy.92, pred[8,5]{0,1:T(8,128)(4,1)S(1)} %copy-done.5), kind=kOutput, calls=%fused_computation.18 | convolution fusion | flops 236122112 | bytes 3842088 | tf_op jit(solution)/shard_map/conv_general_dilated | solution.py:31
  108.4 2.5 %collective-permute-done.9 = f32[128,1,4,32]{0,2,3,1:T(4,128)S(1)} collective-permute-done((f32[128,1,4,32]{0,2,3,1:T(4,128)S(1)}, f32[128,1,4,32]{0,2,3,1:T(4,128)S(1)}, u32[]{:S(2)}, u32[]{:S(2)}) %collective-permute-start.9) | collective-permute-done | bytes 65568 | tf_op jit(solution)/shard_map/ppermute | solution.py:27
  (70 shorter events, 10.0 us)
Async XLA Ops:
  0.0 62.5 %copy-start = (f32[3,3,3,128,128]{4,3,2,1,0:T(8,128)S(1)}, f32[3,3,3,128,128]{4,3,2,1,0:T(8,128)}, u32[]{:S(2)}) copy-start(f32[3,3,3,128,128]{4,3,2,1,0:T(8,128)} %param.17) | copy-start | bytes 5308420
  0.0 6.8 %copy-start.2 = (f32[64,4,4,128]{3,2,1,0:T(4,128)S(1)}, f32[64,4,4,128]{3,2,1,0:T(4,128)}, u32[]{:S(2)}) copy-start(f32[64,4,4,128]{3,2,1,0:T(4,128)} %param.14) | copy-start | bytes 1572868
  1.2 5.6 %collective-permute-start = (f32[64,1,4,128]{3,0,2,1:T(8,128)S(1)}, f32[64,1,4,128]{3,0,2,1:T(8,128)S(1)}, u32[]{:S(2)}, u32[]{:S(2)}) collective-permute-start(f32[64,1,4,128]{3,0,2,1:T(8,128)S(1)} %copy.117), channel_id=1, source_target_pairs={{0,4},{4,8},{8,12},{12,16},{16,20},{20,24},{24,28},{1,5},{5,9},{9,... | collective-permute-start | bytes 393224 | tf_op jit(solution)/shard_map/ppermute | solution.py:15
  4.9 7.2 %collective-permute-start.1 = (f32[64,1,4,128]{3,0,2,1:T(8,128)S(1)}, f32[64,1,4,128]{3,0,2,1:T(8,128)S(1)}, u32[]{:S(2)}, u32[]{:S(2)}) collective-permute-start(f32[64,1,4,128]{3,0,2,1:T(8,128)S(1)} %copy.118), channel_id=1, source_target_pairs={{4,0},{8,4},{12,8},{16,12},{20,16},{24,20},{28,24},{5,1},{9,5},{13... | collective-permute-start | bytes 393224 | tf_op jit(solution)/shard_map/ppermute | solution.py:17
  12.1 6.3 %collective-permute-start.2 = (f32[64,6,1,128]{3,0,2,1:T(8,128)S(1)}, f32[64,6,1,128]{3,0,2,1:T(8,128)S(1)}, u32[]{:S(2)}, u32[]{:S(2)}) collective-permute-start(f32[64,6,1,128]{3,0,2,1:T(8,128)S(1)} %get-tuple-element.45), channel_id=1, source_target_pairs={{0,1},{1,2},{2,3},{4,5},{5,6},{6,7},{8,9},{9,10},{10,11},{12,13},{... | collective-permute-start | bytes 589832 | tf_op jit(solution)/shard_map/ppermute | solution.py:15
  15.3 7.1 %collective-permute-start.3 = (f32[64,6,1,128]{3,0,2,1:T(8,128)S(1)}, f32[64,6,1,128]{3,0,2,1:T(8,128)S(1)}, u32[]{:S(2)}, u32[]{:S(2)}) collective-permute-start(f32[64,6,1,128]{3,0,2,1:T(8,128)S(1)} %get-tuple-element.46), channel_id=1, source_target_pairs={{1,0},{2,1},{3,2},{5,4},{6,5},{7,6},{9,8},{10,9},{11,10},{13,12},{... | collective-permute-start | bytes 589832 | tf_op jit(solution)/shard_map/ppermute | solution.py:17
  30.2 1.2 %copy-start.7 = (f32[3,3,3,64,64]{4,3,2,1,0:T(8,128)S(1)}, f32[3,3,3,64,64]{4,3,2,1,0:T(8,128)}, u32[]{:S(2)}) copy-start(f32[3,3,3,64,64]{4,3,2,1,0:T(8,128)} %param.15) | copy-start | bytes 1327108
  30.2 1.2 %copy-start.8 = (pred[8,17]{0,1:T(8,128)(4,1)S(1)}, pred[8,17]{0,1:T(8,128)(4,1)}, u32[]{:S(2)}) copy-start(pred[8,17]{0,1:T(8,128)(4,1)} %constant.216) | copy-start | bytes 412
  40.6 1.0 copy-start.4
  42.2 6.1 %collective-permute-start.4 = (f32[128,1,2,64]{0,3,2,1:T(8,128)S(1)}, f32[128,1,2,64]{0,3,2,1:T(8,128)S(1)}, u32[]{:S(2)}, u32[]{:S(2)}) collective-permute-start(f32[128,1,2,64]{0,3,2,1:T(8,128)S(1)} %get-tuple-element.53), channel_id=1, source_target_pairs={{0,4},{4,8},{8,12},{12,16},{16,20},{20,24},{24,28},{1,5},{5,9},{9,... | collective-permute-start | bytes 196616 | tf_op jit(solution)/shard_map/ppermute | solution.py:15
  46.4 6.5 %collective-permute-start.5 = (f32[128,1,2,64]{0,3,2,1:T(8,128)S(1)}, f32[128,1,2,64]{0,3,2,1:T(8,128)S(1)}, u32[]{:S(2)}, u32[]{:S(2)}) collective-permute-start(f32[128,1,2,64]{0,3,2,1:T(8,128)S(1)} %get-tuple-element.54), channel_id=1, source_target_pairs={{4,0},{8,4},{12,8},{16,12},{20,16},{24,20},{28,24},{5,1},{9,5},{13... | collective-permute-start | bytes 196616 | tf_op jit(solution)/shard_map/ppermute | solution.py:17
  52.9 5.1 %collective-permute-start.6 = (f32[128,4,1,64]{0,3,2,1:T(8,128)S(1)}, f32[128,4,1,64]{0,3,2,1:T(8,128)S(1)}, u32[]{:S(2)}, u32[]{:S(2)}) collective-permute-start(f32[128,4,1,64]{0,3,2,1:T(8,128)S(1)} %get-tuple-element.49), channel_id=1, source_target_pairs={{0,1},{1,2},{2,3},{4,5},{5,6},{6,7},{8,9},{9,10},{10,11},{12,13},{... | collective-permute-start | bytes 393224 | tf_op jit(solution)/shard_map/ppermute | solution.py:15
  56.2 5.7 %collective-permute-start.7 = (f32[128,4,1,64]{0,3,2,1:T(8,128)S(1)}, f32[128,4,1,64]{0,3,2,1:T(8,128)S(1)}, u32[]{:S(2)}, u32[]{:S(2)}) collective-permute-start(f32[128,4,1,64]{0,3,2,1:T(8,128)S(1)} %get-tuple-element.50), channel_id=1, source_target_pairs={{1,0},{2,1},{3,2},{5,4},{6,5},{7,6},{9,8},{10,9},{11,10},{13,12},{... | collective-permute-start | bytes 393224 | tf_op jit(solution)/shard_map/ppermute | solution.py:17
  62.3 0.7 copy-start.6
  65.1 14.0 %copy-start.3 = (f32[2,2,2,128,64]{3,4,2,1,0:T(8,128)S(1)}, f32[2,2,2,128,64]{3,4,2,1,0:T(8,128)}, u32[]{:S(2)}) copy-start(f32[2,2,2,128,64]{3,4,2,1,0:T(8,128)} %param.18) | copy-start | bytes 786436
  79.5 13.2 %copy-start.5 = (pred[8,5]{0,1:T(8,128)(4,1)S(1)}, pred[8,5]{0,1:T(8,128)(4,1)}, u32[]{:S(2)}) copy-start(pred[8,5]{0,1:T(8,128)(4,1)} %constant.213) | copy-start | bytes 124
  92.7 13.6 %copy-start.1 = (f32[3,3,3,256,128]{4,3,2,1,0:T(8,128)S(1)}, f32[3,3,3,256,128]{4,3,2,1,0:T(8,128)}, u32[]{:S(2)}) copy-start(f32[3,3,3,256,128]{4,3,2,1,0:T(8,128)} %param.19) | copy-start | bytes 10616836
  97.0 11.3 %collective-permute-start.8 = (f32[128,1,4,32]{0,2,3,1:T(4,128)S(1)}, f32[128,1,4,32]{0,2,3,1:T(4,128)S(1)}, u32[]{:S(2)}, u32[]{:S(2)}) collective-permute-start(f32[128,1,4,32]{0,2,3,1:T(4,128)S(1)} %slice_bitcast_fusion.1), channel_id=1, source_target_pairs={{0,4},{4,8},{8,12},{12,16},{16,20},{20,24},{24,28},{1,5},{5,9},{9,... | collective-permute-start | bytes 196616 | tf_op jit(solution)/shard_map/ppermute | solution.py:27
  104.4 6.5 %collective-permute-start.9 = (f32[128,1,4,32]{0,2,3,1:T(4,128)S(1)}, f32[128,1,4,32]{0,2,3,1:T(4,128)S(1)}, u32[]{:S(2)}, u32[]{:S(2)}) collective-permute-start(f32[128,1,4,32]{0,2,3,1:T(4,128)S(1)} %slice_bitcast_fusion), channel_id=1, source_target_pairs={{4,0},{8,4},{12,8},{16,12},{20,16},{24,20},{28,24},{5,1},{9,5},{13... | collective-permute-start | bytes 196616 | tf_op jit(solution)/shard_map/ppermute | solution.py:27
where the time goes:
time: 112 us
  starting transfers between devices  29.9 us (27%)
  blocking collectives  26.6 us (24%)
  waiting for transfers between devices  22.4 us (20%)
  matrix products  17.7 us (16%)
  local copies, waits for them, and re-layouts  14 us (12%)
    conv_general_dilated x7, matrix products, convolve(): lax.conv_general_dilated(field[None], kernel, (stride, stride, stride), p...  17.7 us
    ppermute x4, waiting for transfers between devices, padded_2(): lax.ppermute(head, axis, [((i + 1) % count, i) for i in range(ends)])  17.5 us
    ppermute x4, starting transfers between devices, padded_2(): lax.ppermute(tail, axis, [(i, (i + 1) % count) for i in range(ends)])  14.3 us
    all_gather x1, blocking collectives, per_device(): gathered = lax.all_gather(level_two, 'grp', axis=2, tiled=True)  13.8 us
    all_gather x1, blocking collectives, per_device(): coarse = lax.all_gather(shares, 'grp', axis=0, tiled=True)  12.8 us
    ppermute x2, starting transfers between devices, from_behind(): return lax.ppermute(shard, axis, pairs)  9.24 us
    unnamed x25, local copies, waits for them, and re-layouts  6.57 us
    ppermute x4, starting transfers between devices, padded_2(): lax.ppermute(head, axis, [((i + 1) % count, i) for i in range(ends)])  6.43 us
  transfers between devices with their start and end apart: 10, of which 7 were waited for; matrix products, arithmetic and copies ran while one was open for 2% of the time, Pallas kernels for 0%

commit v1 on v0

--- a/solution.py
+++ b/solution.py
@@ -46,7 +46,8 @@
     level_two = convolve(level_one, down_first, 2, valid)
     padded_two = padded_2(level_two, (("slab", 1), ("grp", 2)), 1)
     level_two = jax.nn.gelu(convolve(padded_two, conv_middle, 1, sideways), approximate=False)
-    gathered = lax.all_gather(level_two, "grp", axis=2, tiled=True)
+    blocks = lax.all_gather(level_two, "grp")
+    gathered = jnp.concatenate(blocks, axis=2)
     shares = convolve(gathered, down_second, 2, valid)
     coarse = lax.all_gather(shares, "grp", axis=0, tiled=True)
     planar = ((0, 0), (1, 1), (1, 1))

time: 112 us -> 113 us (level)
  no operation moved by 1% of the time
where the time goes in v1:
time: 113 us
  starting transfers between devices  29.9 us (26%)
  blocking collectives  26.5 us (23%)
  waiting for transfers between devices  22.4 us (20%)
  matrix products  18 us (16%)
  local copies, waits for them, and re-layouts  14.7 us (13%)
    conv_general_dilated x7, matrix products, convolve(): lax.conv_general_dilated(field[None], kernel, (stride, stride, stride), p...  18 us
    ppermute x4, waiting for transfers between devices, padded_2(): lax.ppermute(head, axis, [((i + 1) % count, i) for i in range(ends)])  17.5 us
    ppermute x4, starting transfers between devices, padded_2(): lax.ppermute(tail, axis, [(i, (i + 1) % count) for i in range(ends)])  14.3 us
    all_gather x1, blocking collectives, per_device(): blocks = lax.all_gather(level_two, 'grp')  13.7 us
    all_gather x1, blocking collectives, per_device(): coarse = lax.all_gather(shares, 'grp', axis=0, tiled=True)  12.8 us
    ppermute x2, starting transfers between devices, from_behind(): return lax.ppermute(shard, axis, pairs)  9.25 us
    unnamed x25, local copies, waits for them, and re-layouts  7.37 us
    ppermute x4, starting transfers between devices, padded_2(): lax.ppermute(head, axis, [((i + 1) % count, i) for i in range(ends)])  6.43 us
  transfers between devices with their start and end apart: 10, of which 7 were waited for; matrix products, arithmetic and copies ran while one was open for 2% of the time, Pallas kernels for 0%

profile of v1, /device:TPU:3, one launch (start us, length us, event | category | flops | bytes accessed | tf_op | source)
XLA Modules:
  0.0 112.5 jit_solution(2615987414007153775)
XLA Ops:
  1.2 3.7 %collective-permute-start = (f32[64,1,4,128]{3,0,2,1:T(8,128)S(1)}, f32[64,1,4,128]{3,0,2,1:T(8,128)S(1)}, u32[]{:S(2)}, u32[]{:S(2)}) collective-permute-start(f32[64,1,4,128]{3,0,2,1:T(8,128)S(1)} %copy.71), channel_id=1, source_target_pairs={{0,4},{4,8},{8,12},{12,16},{16,20},{20,24},{24,28},{1,5},{5,9},{9,... | collective-permute-start | bytes 393224 | tf_op jit(solution)/shard_map/ppermute | solution.py:15
  4.9 1.9 %collective-permute-start.1 = (f32[64,1,4,128]{3,0,2,1:T(8,128)S(1)}, f32[64,1,4,128]{3,0,2,1:T(8,128)S(1)}, u32[]{:S(2)}, u32[]{:S(2)}) collective-permute-start(f32[64,1,4,128]{3,0,2,1:T(8,128)S(1)} %copy.72), channel_id=1, source_target_pairs={{4,0},{8,4},{12,8},{16,12},{20,16},{24,20},{28,24},{5,1},{9,5},{13... | collective-permute-start | bytes 393224 | tf_op jit(solution)/shard_map/ppermute | solution.py:17
  7.0 5.1 %collective-permute-done.1 = f32[64,1,4,128]{3,0,2,1:T(8,128)S(1)} collective-permute-done((f32[64,1,4,128]{3,0,2,1:T(8,128)S(1)}, f32[64,1,4,128]{3,0,2,1:T(8,128)S(1)}, u32[]{:S(2)}, u32[]{:S(2)}) %collective-permute-start.1) | collective-permute-done | bytes 131104 | tf_op jit(solution)/shard_map/ppermute | solution.py:17
  12.1 3.2 %collective-permute-start.2 = (f32[64,6,1,128]{3,0,2,1:T(8,128)S(1)}, f32[64,6,1,128]{3,0,2,1:T(8,128)S(1)}, u32[]{:S(2)}, u32[]{:S(2)}) collective-permute-start(f32[64,6,1,128]{3,0,2,1:T(8,128)S(1)} %get-tuple-element.45), channel_id=1, source_target_pairs={{0,1},{1,2},{2,3},{4,5},{5,6},{6,7},{8,9},{9,10},{10,11},{12,13},{... | collective-permute-start | bytes 589832 | tf_op jit(solution)/shard_map/ppermute | solution.py:15
  16.6 1.7 %collective-permute-done.2 = f32[64,6,1,128]{3,0,2,1:T(8,128)S(1)} collective-permute-done((f32[64,6,1,128]{3,0,2,1:T(8,128)S(1)}, f32[64,6,1,128]{3,0,2,1:T(8,128)S(1)}, u32[]{:S(2)}, u32[]{:S(2)}) %collective-permute-start.2) | collective-permute-done | bytes 196640 | tf_op jit(solution)/shard_map/ppermute | solution.py:15
  18.4 4.1 %collective-permute-done.3 = f32[64,6,1,128]{3,0,2,1:T(8,128)S(1)} collective-permute-done((f32[64,6,1,128]{3,0,2,1:T(8,128)S(1)}, f32[64,6,1,128]{3,0,2,1:T(8,128)S(1)}, u32[]{:S(2)}, u32[]{:S(2)}) %collective-permute-start.3) | collective-permute-done | bytes 196640 | tf_op jit(solution)/shard_map/ppermute | solution.py:17
  22.6 4.3 %copy.66 = f32[64,6,6,1,128]{0,3,4,2,1:T(1,128)} copy(f32[64,6,6,1,128]{4,0,2,1,3:T(8,128)S(1)} %maximum_bitcast_fusion) | data formatting | bytes 2359296
  26.9 3.4 %pad.6.clone = f32[64,6,6,1,136]{0,3,4,2,1:T(1,128)S(1)} pad(f32[64,6,6,1,128]{0,3,4,2,1:T(1,128)} %copy.66, f32[]{:T(128)} %constant.74.clone.1), padding=0_0x0_0x0_0x0_0x1_7 | pad | bytes 2433028 | tf_op jit(solution)/shard_map/broadcast_in_dim | solution.py:32
  31.4 8.9 %fusion.22 = f32[4,4,8,17,64]{4,2,3,1,0:T(8,128)S(1)} fusion(f32[3,3,3,64,64]{4,3,2,1,0:T(8,128)S(1)} %copy-done.6, f32[64,6,6,1,7,2]{0,4,5,2,1,3:T(8,128)S(1)} %slice.106, f32[64,6,6,1,8,17]{0,4,5,2,1,3:T(8,128)S(1)} %copy.38, pred[8,17]{0,1:T(8,128)(4,1)S(1)} %copy-done.7), kind=kOutput, calls=%fused_computation.21 | convolution fusion | flops 1454131200 | bytes 2381960 | tf_op jit(solution)/shard_map/conv_general_dilated | solution.py:31
  42.3 4.2 %collective-permute-start.4 = (f32[128,1,2,64]{0,3,2,1:T(8,128)S(1)}, f32[128,1,2,64]{0,3,2,1:T(8,128)S(1)}, u32[]{:S(2)}, u32[]{:S(2)}) collective-permute-start(f32[128,1,2,64]{0,3,2,1:T(8,128)S(1)} %get-tuple-element.51), channel_id=1, source_target_pairs={{0,4},{4,8},{8,12},{12,16},{16,20},{20,24},{24,28},{1,5},{5,9},{9,... | collective-permute-start | bytes 196616 | tf_op jit(solution)/shard_map/ppermute | solution.py:15
  46.4 1.9 %collective-permute-start.5 = (f32[128,1,2,64]{0,3,2,1:T(8,128)S(1)}, f32[128,1,2,64]{0,3,2,1:T(8,128)S(1)}, u32[]{:S(2)}, u32[]{:S(2)}) collective-permute-start(f32[128,1,2,64]{0,3,2,1:T(8,128)S(1)} %get-tuple-element.52), channel_id=1, source_target_pairs={{4,0},{8,4},{12,8},{16,12},{20,16},{24,20},{28,24},{5,1},{9,5},{13... | collective-permute-start | bytes 196616 | tf_op jit(solution)/shard_map/ppermute | solution.py:17
  48.4 4.5 %collective-permute-done.5 = f32[128,1,2,64]{0,3,2,1:T(8,128)S(1)} collective-permute-done((f32[128,1,2,64]{0,3,2,1:T(8,128)S(1)}, f32[128,1,2,64]{0,3,2,1:T(8,128)S(1)}, u32[]{:S(2)}, u32[]{:S(2)}) %collective-permute-start.5) | collective-permute-done | bytes 65568 | tf_op jit(solution)/shard_map/ppermute | solution.py:17
  53.0 3.2 %collective-permute-start.6 = (f32[128,4,1,64]{0,3,2,1:T(8,128)S(1)}, f32[128,4,1,64]{0,3,2,1:T(8,128)S(1)}, u32[]{:S(2)}, u32[]{:S(2)}) collective-permute-start(f32[128,4,1,64]{0,3,2,1:T(8,128)S(1)} %get-tuple-element.49), channel_id=1, source_target_pairs={{0,1},{1,2},{2,3},{4,5},{5,6},{6,7},{8,9},{9,10},{10,11},{12,13},{... | collective-permute-start | bytes 393224 | tf_op jit(solution)/shard_map/ppermute | solution.py:15
  56.2 1.3 %collective-permute-start.7 = (f32[128,4,1,64]{0,3,2,1:T(8,128)S(1)}, f32[128,4,1,64]{0,3,2,1:T(8,128)S(1)}, u32[]{:S(2)}, u32[]{:S(2)}) collective-permute-start(f32[128,4,1,64]{0,3,2,1:T(8,128)S(1)} %get-tuple-element.50), channel_id=1, source_target_pairs={{1,0},{2,1},{3,2},{5,4},{6,5},{7,6},{9,8},{10,9},{11,10},{13,12},{... | collective-permute-start | bytes 393224 | tf_op jit(solution)/shard_map/ppermute | solution.py:17
  58.1 3.8 %collective-permute-done.7 = f32[128,4,1,64]{0,3,2,1:T(8,128)S(1)} collective-permute-done((f32[128,4,1,64]{0,3,2,1:T(8,128)S(1)}, f32[128,4,1,64]{0,3,2,1:T(8,128)S(1)}, u32[]{:S(2)}, u32[]{:S(2)}) %collective-permute-start.7) | collective-permute-done | bytes 131104 | tf_op jit(solution)/shard_map/ppermute | solution.py:17
  63.0 2.0 %fusion.55 = f32[2,2,8,9,128]{4,2,3,1,0:T(8,128)S(1)} fusion(f32[3,3,3,128,128]{4,3,2,1,0:T(8,128)S(1)} %copy-done, f32[128,4,4,1,7,2]{0,4,5,2,1,3:T(8,128)S(1)} %slice.113, f32[128,4,4,1,8,9]{0,4,5,2,1,3:T(8,128)S(1)} %copy.46, pred[8,9]{0,1:T(8,128)(4,1)S(1)} %copy-done.8), kind=kOutput, calls=%fused_computation.67 | convolution fusion | flops 767348736 | bytes 2621512 | tf_op jit(solution)/shard_map/conv_general_dilated | solution.py:31
  65.1 13.7 %all_gather.7 = f32[4,128,2,2,64]{1,4,3,2,0:T(8,128)S(1)} all-gather(f32[1,128,2,2,64]{1,4,3,2,0:T(8,128)S(1)} %copy.48), channel_id=1, replica_groups=mesh['slab'=8,'grp'=4] {'grp'}, dimensions={0}, use_global_device_ids=true | all-gather | bytes 655360 | tf_op jit(solution)/shard_map/all_gather | solution.py:49
  80.3 12.8 %all-gather = f32[1,256,1,4,32]{4,3,2,0,1:T(4,128)S(1)} all-gather(f32[1,64,1,4,32]{4,3,2,0,1:T(4,128)S(1)} %copy.53), channel_id=2, replica_groups=mesh['slab'=8,'grp'=4] {'grp'}, dimensions={1}, use_global_device_ids=true | all-gather | bytes 163840 | tf_op jit(solution)/shard_map/all_gather | solution.py:52
  93.4 2.2 %fusion.14 = f32[1,4,8,5,128]{4,2,3,1,0:T(8,128)S(1)} fusion(f32[3,3,3,256,128]{4,3,2,1,0:T(8,128)} %param.19, f32[256,1,4,1,7,2]{0,4,5,2,3,1:T(8,128)S(1)} %slice.116, f32[256,1,4,1,8,5]{0,4,5,2,3,1:T(8,128)S(1)} %copy.56, pred[8,5]{0,1:T(8,128)(4,1)S(1)} %copy-done.5), kind=kOutput, calls=%fused_computation.16 | convolution fusion | flops 236122112 | bytes 1482792 | tf_op jit(solution)/shard_map/conv_general_dilated | solution.py:31
  95.5 2.0 %fusion.17 = f32[1,4,8,5,128]{4,2,3,1,0:T(8,128)S(1)} fusion(f32[3,3,3,256,128]{4,3,2,1,0:T(8,128)} %param.19, f32[256,1,4,1,7,2]{0,4,5,2,3,1:T(8,128)S(1)} %slice.116, f32[256,1,4,1,8,5]{0,4,5,2,3,1:T(8,128)S(1)} %copy.56, pred[8,5]{0,1:T(8,128)(4,1)S(1)} %copy-done.5), kind=kOutput, calls=%fused_computation.17 | convolution fusion | flops 236122112 | bytes 1482792 | tf_op jit(solution)/shard_map/conv_general_dilated | solution.py:31
  97.6 7.3 %collective-permute-start.8 = (f32[128,1,4,32]{0,2,3,1:T(4,128)S(1)}, f32[128,1,4,32]{0,2,3,1:T(4,128)S(1)}, u32[]{:S(2)}, u32[]{:S(2)}) collective-permute-start(f32[128,1,4,32]{0,2,3,1:T(4,128)S(1)} %slice_bitcast_fusion.2), channel_id=1, source_target_pairs={{0,4},{4,8},{8,12},{12,16},{16,20},{20,24},{24,28},{1,5},{5,9},{9,... | collective-permute-start | bytes 196616 | tf_op jit(solution)/shard_map/ppermute | solution.py:27
  105.0 1.9 %collective-permute-start.9 = (f32[128,1,4,32]{0,2,3,1:T(4,128)S(1)}, f32[128,1,4,32]{0,2,3,1:T(4,128)S(1)}, u32[]{:S(2)}, u32[]{:S(2)}) collective-permute-start(f32[128,1,4,32]{0,2,3,1:T(4,128)S(1)} %slice_bitcast_fusion.1), channel_id=1, source_target_pairs={{4,0},{8,4},{12,8},{16,12},{20,16},{24,20},{28,24},{5,1},{9,5},{13... | collective-permute-start | bytes 196616 | tf_op jit(solution)/shard_map/ppermute | solution.py:27
  106.9 2.0 %convolution_select_fusion.1 = f32[1,4,8,5,128]{4,2,3,1,0:T(8,128)S(1)} fusion(f32[3,3,3,256,128]{4,3,2,1,0:T(8,128)S(1)} %copy-done.1, f32[256,1,4,1,7,2]{0,4,5,2,3,1:T(8,128)S(1)} %slice.116, f32[256,1,4,1,8,5]{0,4,5,2,3,1:T(8,128)S(1)} %copy.56, pred[8,5]{0,1:T(8,128)(4,1)S(1)} %copy-done.5), kind=kOutput, calls=%fused_computation.18 | convolution fusion | flops 236122112 | bytes 3842088 | tf_op jit(solution)/shard_map/conv_general_dilated | solution.py:31
  109.0 2.5 %collective-permute-done.9 = f32[128,1,4,32]{0,2,3,1:T(4,128)S(1)} collective-permute-done((f32[128,1,4,32]{0,2,3,1:T(4,128)S(1)}, f32[128,1,4,32]{0,2,3,1:T(4,128)S(1)}, u32[]{:S(2)}, u32[]{:S(2)}) %collective-permute-start.9) | collective-permute-done | bytes 65568 | tf_op jit(solution)/shard_map/ppermute | solution.py:27
  (68 shorter events, 10.4 us)
Async XLA Ops:
  0.0 62.5 %copy-start = (f32[3,3,3,128,128]{4,3,2,1,0:T(8,128)S(1)}, f32[3,3,3,128,128]{4,3,2,1,0:T(8,128)}, u32[]{:S(2)}) copy-start(f32[3,3,3,128,128]{4,3,2,1,0:T(8,128)} %param.17) | copy-start | bytes 5308420
  0.0 6.8 %copy-start.2 = (f32[64,4,4,128]{3,2,1,0:T(4,128)S(1)}, f32[64,4,4,128]{3,2,1,0:T(4,128)}, u32[]{:S(2)}) copy-start(f32[64,4,4,128]{3,2,1,0:T(4,128)} %param.14) | copy-start | bytes 1572868
  1.2 5.6 %collective-permute-start = (f32[64,1,4,128]{3,0,2,1:T(8,128)S(1)}, f32[64,1,4,128]{3,0,2,1:T(8,128)S(1)}, u32[]{:S(2)}, u32[]{:S(2)}) collective-permute-start(f32[64,1,4,128]{3,0,2,1:T(8,128)S(1)} %copy.71), channel_id=1, source_target_pairs={{0,4},{4,8},{8,12},{12,16},{16,20},{20,24},{24,28},{1,5},{5,9},{9,... | collective-permute-start | bytes 393224 | tf_op jit(solution)/shard_map/ppermute | solution.py:15
  4.9 7.2 %collective-permute-start.1 = (f32[64,1,4,128]{3,0,2,1:T(8,128)S(1)}, f32[64,1,4,128]{3,0,2,1:T(8,128)S(1)}, u32[]{:S(2)}, u32[]{:S(2)}) collective-permute-start(f32[64,1,4,128]{3,0,2,1:T(8,128)S(1)} %copy.72), channel_id=1, source_target_pairs={{4,0},{8,4},{12,8},{16,12},{20,16},{24,20},{28,24},{5,1},{9,5},{13... | collective-permute-start | bytes 393224 | tf_op jit(solution)/shard_map/ppermute | solution.py:17
  12.1 6.3 %collective-permute-start.2 = (f32[64,6,1,128]{3,0,2,1:T(8,128)S(1)}, f32[64,6,1,128]{3,0,2,1:T(8,128)S(1)}, u32[]{:S(2)}, u32[]{:S(2)}) collective-permute-start(f32[64,6,1,128]{3,0,2,1:T(8,128)S(1)} %get-tuple-element.45), channel_id=1, source_target_pairs={{0,1},{1,2},{2,3},{4,5},{5,6},{6,7},{8,9},{9,10},{10,11},{12,13},{... | collective-permute-start | bytes 589832 | tf_op jit(solution)/shard_map/ppermute | solution.py:15
  15.3 7.1 %collective-permute-start.3 = (f32[64,6,1,128]{3,0,2,1:T(8,128)S(1)}, f32[64,6,1,128]{3,0,2,1:T(8,128)S(1)}, u32[]{:S(2)}, u32[]{:S(2)}) collective-permute-start(f32[64,6,1,128]{3,0,2,1:T(8,128)S(1)} %get-tuple-element.46), channel_id=1, source_target_pairs={{1,0},{2,1},{3,2},{5,4},{6,5},{7,6},{9,8},{10,9},{11,10},{13,12},{... | collective-permute-start | bytes 589832 | tf_op jit(solution)/shard_map/ppermute | solution.py:17
  30.2 1.2 %copy-start.6 = (f32[3,3,3,64,64]{4,3,2,1,0:T(8,128)S(1)}, f32[3,3,3,64,64]{4,3,2,1,0:T(8,128)}, u32[]{:S(2)}) copy-start(f32[3,3,3,64,64]{4,3,2,1,0:T(8,128)} %param.15) | copy-start | bytes 1327108
  30.2 1.2 %copy-start.7 = (pred[8,17]{0,1:T(8,128)(4,1)S(1)}, pred[8,17]{0,1:T(8,128)(4,1)}, u32[]{:S(2)}) copy-start(pred[8,17]{0,1:T(8,128)(4,1)} %constant.216) | copy-start | bytes 412
  40.7 1.0 copy-start.4
  42.3 6.1 %collective-permute-start.4 = (f32[128,1,2,64]{0,3,2,1:T(8,128)S(1)}, f32[128,1,2,64]{0,3,2,1:T(8,128)S(1)}, u32[]{:S(2)}, u32[]{:S(2)}) collective-permute-start(f32[128,1,2,64]{0,3,2,1:T(8,128)S(1)} %get-tuple-element.51), channel_id=1, source_target_pairs={{0,4},{4,8},{8,12},{12,16},{16,20},{20,24},{24,28},{1,5},{5,9},{9,... | collective-permute-start | bytes 196616 | tf_op jit(solution)/shard_map/ppermute | solution.py:15
  46.4 6.5 %collective-permute-start.5 = (f32[128,1,2,64]{0,3,2,1:T(8,128)S(1)}, f32[128,1,2,64]{0,3,2,1:T(8,128)S(1)}, u32[]{:S(2)}, u32[]{:S(2)}) collective-permute-start(f32[128,1,2,64]{0,3,2,1:T(8,128)S(1)} %get-tuple-element.52), channel_id=1, source_target_pairs={{4,0},{8,4},{12,8},{16,12},{20,16},{24,20},{28,24},{5,1},{9,5},{13... | collective-permute-start | bytes 196616 | tf_op jit(solution)/shard_map/ppermute | solution.py:17
  53.0 5.1 %collective-permute-start.6 = (f32[128,4,1,64]{0,3,2,1:T(8,128)S(1)}, f32[128,4,1,64]{0,3,2,1:T(8,128)S(1)}, u32[]{:S(2)}, u32[]{:S(2)}) collective-permute-start(f32[128,4,1,64]{0,3,2,1:T(8,128)S(1)} %get-tuple-element.49), channel_id=1, source_target_pairs={{0,1},{1,2},{2,3},{4,5},{5,6},{6,7},{8,9},{9,10},{10,11},{12,13},{... | collective-permute-start | bytes 393224 | tf_op jit(solution)/shard_map/ppermute | solution.py:15
  56.2 5.7 %collective-permute-start.7 = (f32[128,4,1,64]{0,3,2,1:T(8,128)S(1)}, f32[128,4,1,64]{0,3,2,1:T(8,128)S(1)}, u32[]{:S(2)}, u32[]{:S(2)}) collective-permute-start(f32[128,4,1,64]{0,3,2,1:T(8,128)S(1)} %get-tuple-element.50), channel_id=1, source_target_pairs={{1,0},{2,1},{3,2},{5,4},{6,5},{7,6},{9,8},{10,9},{11,10},{13,12},{... | collective-permute-start | bytes 393224 | tf_op jit(solution)/shard_map/ppermute | solution.py:17
  62.3 0.7 copy-start.8
  78.8 1.0 copy-start.3
  80.1 13.2 %copy-start.5 = (pred[8,5]{0,1:T(8,128)(4,1)S(1)}, pred[8,5]{0,1:T(8,128)(4,1)}, u32[]{:S(2)}) copy-start(pred[8,5]{0,1:T(8,128)(4,1)} %constant.213) | copy-start | bytes 124
  93.3 13.6 %copy-start.1 = (f32[3,3,3,256,128]{4,3,2,1,0:T(8,128)S(1)}, f32[3,3,3,256,128]{4,3,2,1,0:T(8,128)}, u32[]{:S(2)}) copy-start(f32[3,3,3,256,128]{4,3,2,1,0:T(8,128)} %param.19) | copy-start | bytes 10616836
  97.6 11.3 %collective-permute-start.8 = (f32[128,1,4,32]{0,2,3,1:T(4,128)S(1)}, f32[128,1,4,32]{0,2,3,1:T(4,128)S(1)}, u32[]{:S(2)}, u32[]{:S(2)}) collective-permute-start(f32[128,1,4,32]{0,2,3,1:T(4,128)S(1)} %slice_bitcast_fusion.2), channel_id=1, source_target_pairs={{0,4},{4,8},{8,12},{12,16},{16,20},{20,24},{24,28},{1,5},{5,9},{9,... | collective-permute-start | bytes 196616 | tf_op jit(solution)/shard_map/ppermute | solution.py:27
  105.0 6.5 %collective-permute-start.9 = (f32[128,1,4,32]{0,2,3,1:T(4,128)S(1)}, f32[128,1,4,32]{0,2,3,1:T(4,128)S(1)}, u32[]{:S(2)}, u32[]{:S(2)}) collective-permute-start(f32[128,1,4,32]{0,2,3,1:T(4,128)S(1)} %slice_bitcast_fusion.1), channel_id=1, source_target_pairs={{4,0},{8,4},{12,8},{16,12},{20,16},{24,20},{28,24},{5,1},{9,5},{13... | collective-permute-start | bytes 196616 | tf_op jit(solution)/shard_map/ppermute | solution.py:27
